TPU v7x, 512 devices: a whole 4x8x8 slice. The times are simulated.
512 devices in a mesh: dp: 32 (over x, y), seq: 16 (over z, core).
Axes of the slice: x: 4, y: 8, z: 8, core: 2. Of those that a mesh axis runs over, the one named last changes fastest.
Arguments:
- residual_stream: bfloat16 [262144, 2048], P(('dp', 'seq')), parts along dimension 0, may hold values from -6 to 6
- octet_readout: bfloat16 [256, 2048], replicated, may hold values from -6 to 6
- downsampling_filter: bfloat16 [32, 256, 96], replicated, may hold values from -0.375 to 0.375
- sharpness_factor: float32 [8], replicated, may hold values from 4 to 20
- widening_filter: bfloat16 [32, 32, 256], replicated, may hold values from -2 to 2
Outputs:
- logits: bfloat16 [262144, 256], P(('dp', 'seq')), parts along dimension 0
There are 32 independent parts, one for each index of `dp`. A program takes and returns all parts, laid end to end along the dimension named above; an argument that names none is the same for every part. Nothing has to cross between parts.
All inputs are finite; a program needn't handle non-finite values.
Results may differ from a plain program's by a relative error of at most 0.0052.
Values may be sent and summed in bfloat16 or wider, within the bound.
A program may use at most 64 MiB of HBM per device.

v0:
```python
import jax
import jax.numpy as jnp
from jax import lax
from jax.sharding import PartitionSpec as P

SHORTEN = 4


def shifted_2(array, axis, by):
    count = lax.axis_size(axis)
    pairs = [(i, i + by) for i in range(count) if 0 <= i + by < count]
    return lax.ppermute(array, axis, pairs)


def passed_along(block, axis, distance):
    devices = range(lax.axis_size(axis))
    route = [((i - distance) % len(devices), i) for i in devices]
    return lax.ppermute(block, axis, route)


def normalize(vectors):
    return vectors * lax.rsqrt(jnp.sum(vectors * vectors, axis=-1, keepdims=True) + 1e-06)


def shorten(shifted, kernel_part, groups):
    byte_rows, model_width = shifted.shape
    windows = shifted.reshape(byte_rows // SHORTEN, SHORTEN, groups, model_width // groups)
    kernel = kernel_part.reshape(groups, SHORTEN, model_width // groups, kernel_part.shape[2])
    return jnp.einsum("jtgc,gtco->jgo", windows, kernel, preferred_element_type=jnp.float32)


def on_device(
    residual_stream, octet_readout, downsampling_filter, sharpness_factor, widening_filter
):
    byte_rows = residual_stream.shape[0]
    model_width = residual_stream.shape[1]
    groups = downsampling_filter.shape[0]
    group_width = model_width // groups
    per_group = downsampling_filter.shape[2] // 3
    attention_number = sharpness_factor.shape[0]
    head_size = groups * per_group // attention_number
    tokens_here = byte_rows // SHORTEN
    rim_rows = SHORTEN - 1
    left_rim = shifted_2(residual_stream[byte_rows - rim_rows :], "seq", 1)
    shifted = jnp.concatenate([left_rim, residual_stream[: byte_rows - rim_rows]], 0)
    mixed_out = shorten(shifted, downsampling_filter, groups)
    queries = normalize(
        mixed_out[:, :, :per_group].reshape(tokens_here, attention_number, head_size)
    ).astype(jnp.bfloat16)
    key_unit = normalize(
        mixed_out[:, :, per_group : 2 * per_group].reshape(tokens_here, attention_number, head_size)
    ).astype(jnp.bfloat16)
    values = (
        mixed_out[:, :, 2 * per_group :]
        .reshape(tokens_here, attention_number, head_size)
        .astype(jnp.bfloat16)
    )
    my_index = lax.axis_index("seq")
    first_token = my_index * tokens_here
    sharpness_vertical = sharpness_factor[:, None, None]
    query_pos = first_token + jnp.arange(tokens_here, dtype=jnp.int32)
    stacked = jnp.stack([key_unit, values], 0)
    gathered = lax.all_gather(stacked, "seq", axis=1, tiled=True)
    all_keys, all_values = (gathered[0], gathered[1])
    similarity_matrix = (
        jnp.einsum("jsg,isg->sji", queries, all_keys, preferred_element_type=jnp.float32)
        * sharpness_vertical
    )
    key_pos = jnp.arange(all_keys.shape[0], dtype=jnp.int32)
    future_masked = key_pos[None, :] <= query_pos[:, None]
    softmax_shares = jnp.where(
        future_masked[None],
        jnp.exp(similarity_matrix - sharpness_vertical),
        jnp.zeros((), jnp.float32),
    )
    denom_sum = jnp.sum(softmax_shares, axis=-1)
    weighted = jnp.einsum(
        "hqk,khd->qhd",
        softmax_shares.astype(jnp.bfloat16),
        all_values,
        preferred_element_type=jnp.float32,
    )
    attended = (weighted / jnp.transpose(denom_sum)[:, :, None]).astype(jnp.bfloat16)
    attended = attended.reshape(tokens_here, groups, per_group)
    upsampled = jnp.einsum(
        "jgc,gcu->jgu", attended, widening_filter, preferred_element_type=jnp.float32
    )
    upsampled = (
        upsampled.reshape(tokens_here, groups, SHORTEN, group_width)
        .transpose(0, 2, 1, 3)
        .reshape(byte_rows, model_width)
    )
    hidden = residual_stream.astype(jnp.float32) + upsampled
    normed = (hidden * lax.rsqrt(jnp.mean(hidden * hidden, axis=-1, keepdims=True) + 1e-05)).astype(
        jnp.bfloat16
    )
    logits = lax.dot_general(
        normed, octet_readout, (((1,), (1,)), ((), ())), preferred_element_type=jnp.float32
    ) * model_width ** (-0.5)
    return logits.astype(jnp.bfloat16)


def solution(mesh):
    in_specs = (P(("dp", "seq"), None), P(), P(), P(), P())
    out_specs = P(("dp", "seq"), None)
    return jax.shard_map(
        on_device, mesh=mesh, in_specs=in_specs, out_specs=out_specs, check_vma=False
    )
```

profile of v0, /device:TPU:1, one launch (start us, length us, event | category | flops | bytes accessed | tf_op | source)
XLA Modules:
  0.0 155.1 jit_solution(6165816291397608881)
XLA Ops:
  6.5 0.0 copy-start
  6.5 0.0 copy-start.2
  6.5 0.0 all-gather.2.cloned.1.call-start
  6.5 0.9 slice.22
  7.5 5.5 %collective-permute-start = (bf16[3,2048]{1,0:T(4,128)(2,1)S(1)}, bf16[3,2048]{1,0:T(4,128)(2,1)S(1)}, u32[]{:S(2)}, u32[]{:S(2)}) collective-permute-start(bf16[3,2048]{1,0:T(4,128)(2,1)S(1)} %slice.22), channel_id=1, source_target_pairs={{0,1},{1,2},{2,3},{3,4},{4,5},{5,6},{6,7},{7,8},{8,9},{9,10},{10,1... | collective-permute-start | bytes 36872 | tf_op jit(solution)/shard_map/ppermute | solution.py:12
  13.0 3.9 %copy.12 = bf16[32,256,96]{2,1,0:T(8,128)(2,1)} copy(bf16[32,256,96]{1,2,0:T(8,128)(2,1)} %param.7) | data formatting | bytes 3145728 | tf_op args[2]
  16.8 0.0 collective-permute-done
  16.8 0.0 copy-done.2
  16.9 1.9 %pad_maximum_fusion = bf16[512,2048]{1,0:T(8,128)(2,1)} fusion(bf16[509,2048]{1,0:T(8,128)(2,1)S(1)} %bitcast.45, bf16[3,2048]{1,0:T(4,128)(2,1)S(1)} %collective-permute-done), kind=kLoop, calls=%fused_computation.17 | loop fusion | flops 4194304 | bytes 4194304 | tf_op jit(solution)/shard_map/concatenate | solution.py:45
  18.8 7.1 %reshape.93 = bf16[128,4,32,64]{3,2,1,0:T(8,128)(2,1)} reshape(bf16[512,2048]{1,0:T(8,128)(2,1)} %pad_maximum_fusion) | data formatting | bytes 4194304 | tf_op jit(solution)/shard_map/reshape | solution.py:27
  25.9 7.8 %fusion.12 = f32[128,32,96]{0,2,1:T(8,128)S(1)} fusion(bf16[32,4,64,96]{3,2,1,0:T(8,128)(2,1)} %bitcast.47, bf16[128,4,32,64]{3,2,1,0:T(8,128)(2,1)} %reshape.93), kind=kOutput, calls=%fused_computation.19 | convolution fusion | flops 201326592 | bytes 5242880 | tf_op jit(solution)/shard_map/jtgc,gtco->jgo/dot_general | solution.py:29
  33.7 0.0 copy-start.5
  33.7 1.1 multiply_reduce_fusion.1
  34.9 0.9 copy.15
  35.7 2.1 %copy.14 = f32[1,128,8,128]{3,1,2,0:T(8,128)} copy(f32[1,128,8,128]{1,3,2,0:T(8,128)} %bitcast.49) | data formatting | bytes 1048576 | tf_op jit(solution)/shard_map/reshape | solution.py:51
  37.8 1.2 multiply_convert_fusion.7
  39.0 1.9 %pad_maximum_fusion.1 = bf16[2,128,8,128]{3,1,2,0:T(8,128)(2,1)} fusion(bf16[1,128,8,128]{3,1,2,0:T(8,128)(2,1)} %copy.15, bf16[1,128,8,128]{3,1,2,0:T(8,128)(2,1)S(1)} %multiply_convert_fusion.7), kind=kLoop, calls=%fused_computation.27 | loop fusion | flops 262144 | bytes 1048576 | tf_op jit(solution)/shard_map/stack | solution.py:62
  40.9 0.0 all-gather.2.cloned.1.call-update
  40.9 0.2 iota_compare_fusion
  41.2 2.0 %copy.16 = f32[128,8,128]{2,0,1:T(8,128)} copy(f32[128,8,128]{0,2,1:T(8,128)} %bitcast.48) | data formatting | bytes 1048576 | tf_op jit(solution)/shard_map/reshape | solution.py:48
  43.2 60.8 %all-gather.2.cloned.1.call-done = bf16[2,2048,8,128]{3,1,2,0:T(8,128)(2,1)} async-done(((bf16[2,128,8,128]{3,1,2,0:T(8,128)(2,1)}), bf16[2,2048,8,128]{3,1,2,0:T(8,128)(2,1)}) %all-gather.2.cloned.1.call-update) | async-done | bytes 8388624 | tf_op jit(solution)/shard_map/all_gather | solution.py:63
  104.0 0.0 copy-done.5
  104.0 0.0 copy-start.4
  104.0 8.3 %fusion = (f32[8,128]{1,0:T(8,128)S(1)}, f32[8,128,2048]{2,1,0:T(8,128)}) fusion(f32[8]{0:T(128)S(1)} %copy-done.5, pred[128,2048]{1,0:T(8,128)(4,1)S(1)} %iota_compare_fusion, bf16[2,2048,8,128]{3,1,2,0:T(8,128)(2,1)} %all-gather.2.cloned.1.call-done, f32[128,8,128]{2,0,1:T(8,128)} %copy.16, f32[128,8]{0,1:T(8,128)S(1)} %add_rsqrt_fusion), kind=kOutput, calls=%fused_computation.1 | convolution fusion | flops 545520640 | bytes 13377568 | tf_op jit(solution)/shard_map/jsg,isg->sji/dot_general | solution.py:66
  112.3 0.0 copy-done.4
  112.3 0.0 copy-start.3
  112.3 5.8 %fusion.23 = bf16[128,8,128]{0,2,1:T(8,128)(2,1)S(1)} fusion(f32[8,128,2048]{2,1,0:T(8,128)} %get-tuple-element.10, f32[8]{0:T(128)S(1)} %copy-done.5, pred[128,2048]{1,0:T(8,128)(4,1)S(1)} %iota_compare_fusion, bf16[2,2048,8,128]{3,1,2,0:T(8,128)(2,1)S(1)} %copy-done.4, f32[128,8]{0,1:T(8,128)S(1)} %bitcast.54), kind=kOutput, calls=%fused_computation.25 | convolution fusion | flops 545521664 | bytes 13111808 | tf_op jit(solution)/shard_map/hqk,khd->qhd/dot_general | solution.py:77
  118.1 0.0 copy-done.3
  118.1 2.7 %convolution_bitcast_fusion = f32[128,32,256]{2,0,1:T(8,128)} fusion(bf16[128,32,32]{0,2,1:T(8,128)(2,1)S(1)} %bitcast.51, bf16[32,32,256]{2,1,0:T(8,128)(2,1)S(1)} %copy-done.3), kind=kOutput, calls=%fused_computation.15 | convolution fusion | flops 67108864 | bytes 4980736 | tf_op jit(solution)/shard_map/jgc,gcu->jgu/dot_general | solution.py:85
  120.8 5.6 %copy.18 = f32[128,32,256]{0,2,1:T(8,128)} copy(f32[128,32,256]{2,0,1:T(8,128)} %convolution_bitcast_fusion) | data formatting | bytes 8388608 | tf_op jit(solution)/shard_map/jgc,gcu->jgu/transpose | solution.py:85
  126.4 9.1 %copy.19 = f32[128,4,32,64]{3,2,1,0:T(8,128)} copy(f32[128,4,32,64]{0,3,1,2:T(8,128)} %bitcast.46) | data formatting | bytes 8388608 | tf_op jit(solution)/shard_map/transpose | solution.py:90
  135.5 7.8 %reshape.99 = f32[512,2048]{1,0:T(8,128)} reshape(f32[128,4,32,64]{3,2,1,0:T(8,128)} %copy.19) | data formatting | bytes 8388608 | tf_op jit(solution)/shard_map/reshape | solution.py:91
  143.3 0.0 copy-start.1
  143.3 3.0 %multiply_reduce_fusion = f32[512]{0:T(512)S(1)} fusion(f32[512,2048]{1,0:T(8,128)} %reshape.99, bf16[512,2048]{1,0:T(8,128)(2,1)S(1)} %copy-done.2), kind=kLoop, calls=%fused_computation.10 | loop fusion | flops 4193792 | bytes 6293504 | tf_op jit(solution)/shard_map/reduce_sum | solution.py:94
  146.3 0.0 copy-done
  146.3 0.5 copy-done.1
  146.8 1.5 fusion.19
  (7 shorter events, 0.1 us)
Async XLA Ops:
  6.5 139.8 %copy-start = (bf16[256,2048]{1,0:T(8,128)(2,1)S(1)}, bf16[256,2048]{1,0:T(8,128)(2,1)}, u32[]{:S(2)}) copy-start(bf16[256,2048]{1,0:T(8,128)(2,1)} %param.6) | copy-start | bytes 3145732
  6.5 10.3 %copy-start.2 = (bf16[512,2048]{1,0:T(8,128)(2,1)S(1)}, bf16[512,2048]{1,0:T(8,128)(2,1)}, u32[]{:S(2)}) copy-start(bf16[512,2048]{1,0:T(8,128)(2,1)} %param.5) | copy-start | bytes 6291460
  6.5 97.4 %all-gather.2.cloned.1.call-start = ((), (), s32[]{:S(2)}) async-start(), calls=%async_computation | async-start | bytes 8912896 | tf_op jit(solution)/shard_map/all_gather | solution.py:63
  7.5 9.4 %collective-permute-start = (bf16[3,2048]{1,0:T(4,128)(2,1)S(1)}, bf16[3,2048]{1,0:T(4,128)(2,1)S(1)}, u32[]{:S(2)}, u32[]{:S(2)}) collective-permute-start(bf16[3,2048]{1,0:T(4,128)(2,1)S(1)} %slice.22), channel_id=1, source_target_pairs={{0,1},{1,2},{2,3},{3,4},{4,5},{5,6},{6,7},{7,8},{8,9},{9,10},{10,1... | collective-permute-start | bytes 36872 | tf_op jit(solution)/shard_map/ppermute | solution.py:12
  33.7 70.3 %copy-start.5 = (f32[8]{0:T(128)S(1)}, f32[8]{0:T(128)}, u32[]{:S(2)}) copy-start(f32[8]{0:T(128)} %param.8) | copy-start | bytes 100
  104.0 8.3 %copy-start.4 = (bf16[2,2048,8,128]{3,1,2,0:T(8,128)(2,1)S(1)}, bf16[2,2048,8,128]{3,1,2,0:T(8,128)(2,1)}, u32[]{:S(2)}) copy-start(bf16[2,2048,8,128]{3,1,2,0:T(8,128)(2,1)} %all-gather.2.cloned.1.call-done) | copy-start | bytes 25165828
  112.3 5.9 %copy-start.3 = (bf16[32,32,256]{2,1,0:T(8,128)(2,1)S(1)}, bf16[32,32,256]{2,1,0:T(8,128)(2,1)}, u32[]{:S(2)}) copy-start(bf16[32,32,256]{2,1,0:T(8,128)(2,1)} %param.9) | copy-start | bytes 1572868
  143.3 3.4 %copy-start.1 = (f32[512,2048]{1,0:T(8,128)S(1)}, f32[512,2048]{1,0:T(8,128)}, u32[]{:S(2)}) copy-start(f32[512,2048]{1,0:T(8,128)} %reshape.99) | copy-start | bytes 12582916
Sparse Core Ops, SparseCore 0:
  41.0 62.9 all-gather.1
where the time goes:
time: 156 us; the launch traced here: 155 us
  waiting for transfers between devices  60.8 us (39%)
  local copies, waits for them, and re-layouts  39.9 us (26%)
  matrix products  26.1 us (17%)
  between operations  13.5 us (9%)
  other arithmetic  9.4 us (6%)
  starting transfers between devices  5.51 us (4%)
    all_gather x1, waiting for transfers between devices, on_device(): gathered = lax.all_gather(stacked, 'seq', axis=1, tiled=True)  60.8 us
    transpose x1, local copies, waits for them, and re-layouts, on_device(): upsampled = upsampled.reshape(tokens_here, groups, SHORTEN, group_width)....  9.14 us
    dot_general x1, matrix products, on_device(): jnp.einsum('jsg,isg->sji', queries, all_keys, preferred_element_type=jnp....  8.29 us
    reshape x1, local copies, waits for them, and re-layouts, on_device(): upsampled = upsampled.reshape(tokens_here, groups, SHORTEN, group_width)....  7.82 us
    dot_general x1, matrix products, shorten(): jnp.einsum('jtgc,gtco->jgo', windows, kernel, preferred_element_type=jnp....  7.76 us
    reshape x1, local copies, waits for them, and re-layouts, shorten(): shifted.reshape(byte_rows // SHORTEN, SHORTEN, groups, model_width // gro...  7.08 us
    dot_general x1, matrix products, on_device(): jnp.einsum('hqk,khd->qhd', softmax_shares.astype(jnp.bfloat16), all_value...  5.85 us
    transpose x1, local copies, waits for them, and re-layouts, on_device(): jnp.einsum('jgc,gcu->jgu', attended, widening_filter, preferred_element_t...  5.56 us
  transfers between devices with their start and end apart: 2, of which 1 were waited for; matrix products, arithmetic and copies ran while one was open for 4% of the time, Pallas kernels for 0%

commit v1 on v0

--- a/solution.py
+++ b/solution.py
@@ -60,7 +60,9 @@
     sharpness_vertical = sharpness_factor[:, None, None]
     query_pos = first_token + jnp.arange(tokens_here, dtype=jnp.int32)
     stacked = jnp.stack([key_unit, values], 0)
-    gathered = lax.all_gather(stacked, "seq", axis=1, tiled=True)
+    gathered = jnp.concatenate(
+        lax.all_to_all(jnp.stack([stacked] * lax.axis_size("seq")), "seq", 0, 0), axis=1
+    )
     all_keys, all_values = (gathered[0], gathered[1])
     similarity_matrix = (
         jnp.einsum("jsg,isg->sji", queries, all_keys, preferred_element_type=jnp.float32)

time: 156 us -> 291 us (1.87)
  waiting for transfers between devices: 60.8 us -> 181 us
  local copies, waits for them, and re-layouts: 39.9 us -> 68.1 us
  between operations: 13.5 us -> 0.14 us
  starting transfers between devices: 5.51 us -> 15 us
  matrix products: 26.1 us -> 17.1 us
    all_to_all x0 -> x1, waiting for transfers between devices: none -> 181 us  [on_device(): lax.all_to_all(jnp.stack([stacked] * lax.axis_size('seq')), 'seq', 0, 0)]
    all_gather x1 -> x0, waiting for transfers between devices: 60.8 us -> none  [on_device(): gathered = lax.all_gather(stacked, 'seq', axis=1, tiled=True)]
    slice x0 -> x3, local copies, waits for them, and re-layouts: none -> 15.4 us  [on_device(): all_keys, all_values = (gathered[0], gathered[1])]
    all_to_all x0 -> x1, starting transfers between devices: none -> 9.53 us  [on_device(): lax.all_to_all(jnp.stack([stacked] * lax.axis_size('seq')), 'seq', 0, 0)]
    another operation x0 -> x2, local copies, waits for them, and re-layouts: none -> 8.43 us  [the longest x1 6.39 us: on_device(): jnp.stack([stacked] * lax.axis_size('seq'))]
    squeeze x0 -> x1, local copies, waits for them, and re-layouts: none -> 7.31 us  [on_device(): all_keys, all_values = (gathered[0], gathered[1])]
    dot_general x1, matrix products: 8.29 us -> 3 us  [on_device(): jnp.einsum('jsg,isg->sji', queries, all_keys, preferred_element_type=jnp....]
    dot_general x1, matrix products: 5.85 us -> 2.14 us  [on_device(): jnp.einsum('hqk,khd->qhd', softmax_shares.astype(jnp.bfloat16), all_value...]
  transfers between devices with their start and end apart: 2 -> 2, of which waited for: 1 -> 1; matrix products, arithmetic and copies ran while one was open for 4% -> 2% of each run, Pallas kernels for 0% -> 0%
where the time goes in v1:
time: 291 us; the launch traced here: 290 us
  waiting for transfers between devices  181 us (62%)
  local copies, waits for them, and re-layouts  68.1 us (23%)
  matrix products  17.1 us (6%)
  starting transfers between devices  15 us (5%)
  other arithmetic  8.25 us (3%)
    all_to_all x1, waiting for transfers between devices, on_device(): lax.all_to_all(jnp.stack([stacked] * lax.axis_size('seq')), 'seq', 0, 0)  181 us
    slice x3, local copies, waits for them, and re-layouts, on_device(): all_keys, all_values = (gathered[0], gathered[1])  15.4 us
    all_to_all x1, starting transfers between devices, on_device(): lax.all_to_all(jnp.stack([stacked] * lax.axis_size('seq')), 'seq', 0, 0)  9.53 us
    transpose x1, local copies, waits for them, and re-layouts, on_device(): upsampled = upsampled.reshape(tokens_here, groups, SHORTEN, group_width)....  9.14 us
    reshape x1, local copies, waits for them, and re-layouts, on_device(): upsampled = upsampled.reshape(tokens_here, groups, SHORTEN, group_width)....  7.82 us
    dot_general x1, matrix products, shorten(): jnp.einsum('jtgc,gtco->jgo', windows, kernel, preferred_element_type=jnp....  7.76 us
    squeeze x1, local copies, waits for them, and re-layouts, on_device(): all_keys, all_values = (gathered[0], gathered[1])  7.31 us
    reshape x1, local copies, waits for them, and re-layouts, shorten(): shifted.reshape(byte_rows // SHORTEN, SHORTEN, groups, model_width // gro...  7.08 us
  transfers between devices with their start and end apart: 2, of which 1 were waited for; matrix products, arithmetic and copies ran while one was open for 2% of the time, Pallas kernels for 0%

profile of v1, /device:TPU:1, one launch (start us, length us, event | category | flops | bytes accessed | tf_op | source)
XLA Modules:
  0.0 289.7 jit_solution(10863437891994621171)
XLA Ops:
  0.0 0.0 copy-start
  0.0 0.0 copy-start.2
  0.0 0.9 slice.24
  0.9 5.5 %collective-permute-start = (bf16[3,2048]{1,0:T(4,128)(2,1)S(1)}, bf16[3,2048]{1,0:T(4,128)(2,1)S(1)}, u32[]{:S(2)}, u32[]{:S(2)}) collective-permute-start(bf16[3,2048]{1,0:T(4,128)(2,1)S(1)} %slice.24), channel_id=1, source_target_pairs={{0,1},{1,2},{2,3},{3,4},{4,5},{5,6},{6,7},{7,8},{8,9},{9,10},{10,1... | collective-permute-start | bytes 36872 | tf_op jit(solution)/shard_map/ppermute | solution.py:12
  6.4 3.9 %copy.18 = bf16[32,256,96]{2,1,0:T(8,128)(2,1)} copy(bf16[32,256,96]{1,2,0:T(8,128)(2,1)} %param.7) | data formatting | bytes 3145728 | tf_op args[2]
  10.3 0.0 collective-permute-done
  10.3 0.0 copy-done.2
  10.3 1.9 pad_maximum_fusion
  12.3 7.1 %reshape.103 = bf16[128,4,32,64]{3,2,1,0:T(8,128)(2,1)} reshape(bf16[512,2048]{1,0:T(8,128)(2,1)} %pad_maximum_fusion) | data formatting | bytes 4194304 | tf_op jit(solution)/shard_map/reshape | solution.py:27
  19.3 7.8 %fusion.11 = f32[128,32,96]{0,2,1:T(8,128)S(1)} fusion(bf16[32,4,64,96]{3,2,1,0:T(8,128)(2,1)} %bitcast.42, bf16[128,4,32,64]{3,2,1,0:T(8,128)(2,1)} %reshape.103), kind=kOutput, calls=%fused_computation.16 | convolution fusion | flops 201326592 | bytes 5242880 | tf_op jit(solution)/shard_map/jtgc,gtco->jgo/dot_general | solution.py:29
  27.2 1.2 multiply_reduce_fusion.1
  28.3 1.1 multiply_convert_fusion.7
  29.4 0.8 pad_maximum_fusion.1
  30.3 2.0 copy.20
  32.3 6.4 %stack.5 = bf16[16,2,128,8,128]{4,2,3,1,0:T(8,128)(2,1)} broadcast(bf16[2,128,8,128]{3,1,2,0:T(8,128)(2,1)} %copy.20), dimensions={1,2,3,4} | broadcast | bytes 8912896 | tf_op jit(solution)/shard_map/stack | solution.py:64
  38.7 9.5 %all-to-all-start = ((bf16[16,2,128,8,128]{4,2,3,1,0:T(8,128)(2,1)}), bf16[16,2,128,8,128]{4,2,3,1,0:T(8,128)(2,1)}, u32[]{:S(2)}, u32[]{:S(2)}) async-start(bf16[16,2,128,8,128]{4,2,3,1,0:T(8,128)(2,1)} %stack.5), calls=%async_computation | async-start | bytes 16777216 | tf_op jit(solution)/shard_map/all_to_all | solution.py:64
  48.2 0.2 iota_compare_fusion
  48.5 2.0 copy.22
  50.5 181.1 %all-to-all-done = bf16[16,2,128,8,128]{4,2,3,1,0:T(8,128)(2,1)} async-done(((bf16[16,2,128,8,128]{4,2,3,1,0:T(8,128)(2,1)}), bf16[16,2,128,8,128]{4,2,3,1,0:T(8,128)(2,1)}, u32[]{:S(2)}, u32[]{:S(2)}) %all-to-all-start) | async-done | bytes 8388640 | tf_op jit(solution)/shard_map/all_to_all | solution.py:64
  231.6 6.0 %fusion.28 = (bf16[1,16,128,8,128]{4,2,3,0,1:T(8,128)(2,1)}, bf16[1,16,128,8,128]{4,2,3,0,1:T(8,128)(2,1)}) fusion(bf16[2,16,128,8,128]{4,2,3,0,1:T(8,128)(2,1)} %bitcast.8), kind=kLoop, calls=%fused_computation.36 | loop fusion | bytes 16777216 | tf_op jit(solution)/shard_map/slice | solution.py:66
  237.7 6.8 %copy.21 = bf16[1,16,128,8,128]{2,1,4,3,0:T(8,128)(2,1)} copy(bf16[1,16,128,8,128]{4,2,3,0,1:T(8,128)(2,1)} %get-tuple-element.8) | data formatting | bytes 8388608 | tf_op jit(solution)/shard_map/slice | solution.py:66
  244.4 7.3 %squeeze.6 = bf16[2048,8,128]{0,2,1:T(8,128)(2,1)} reshape(bf16[1,16,128,8,128]{2,1,4,3,0:T(8,128)(2,1)} %copy.21) | data formatting | bytes 8388608 | tf_op jit(solution)/shard_map/squeeze | solution.py:66
  251.8 0.0 copy-start.5
  251.8 0.0 copy-start.6
  251.8 2.6 copy.23
  254.3 0.0 copy-done.5
  254.3 0.0 copy-done.6
  254.3 0.0 copy-start.3
  254.4 3.0 %fusion = (f32[8,128]{1,0:T(8,128)S(1)}, f32[8,128,2048]{2,1,0:T(8,128)S(1)}) fusion(f32[8]{0:T(128)S(1)} %copy-done.6, pred[128,2048]{1,0:T(8,128)(4,1)S(1)} %iota_compare_fusion, bf16[2048,8,128]{2,0,1:T(8,128)(2,1)S(1)} %bitcast.41, f32[128,8,128]{2,0,1:T(8,128)S(1)} %copy-done.5, f32[128,8]{0,1:T(8,128)S(1)} %add_rsqrt_fusion), kind=kOutput, calls=%fused_computation.1 | convolution fusion | flops 545520640 | bytes 13377568 | tf_op jit(solution)/shard_map/jsg,isg->sji/dot_general | solution.py:68
  257.4 0.0 copy-done.3
  257.4 0.0 copy-start.4
  257.4 2.1 fusion.22
  259.5 0.0 copy-done.4
  259.5 2.7 convolution_bitcast_fusion
  262.2 5.6 %copy.24 = f32[128,32,256]{0,2,1:T(8,128)} copy(f32[128,32,256]{2,0,1:T(8,128)} %convolution_bitcast_fusion) | data formatting | bytes 8388608 | tf_op jit(solution)/shard_map/jgc,gcu->jgu/transpose | solution.py:87
  267.8 9.1 %copy.25 = f32[128,4,32,64]{3,2,1,0:T(8,128)} copy(f32[128,4,32,64]{0,3,1,2:T(8,128)} %bitcast.40) | data formatting | bytes 8388608 | tf_op jit(solution)/shard_map/transpose | solution.py:92
  276.9 7.8 %reshape.110 = f32[512,2048]{1,0:T(8,128)} reshape(f32[128,4,32,64]{3,2,1,0:T(8,128)} %copy.25) | data formatting | bytes 8388608 | tf_op jit(solution)/shard_map/reshape | solution.py:93
  284.7 0.0 copy-start.1
  284.7 3.0 %multiply_reduce_fusion = f32[512]{0:T(512)S(1)} fusion(f32[512,2048]{1,0:T(8,128)} %reshape.110, bf16[512,2048]{1,0:T(8,128)(2,1)S(1)} %copy-done.2), kind=kLoop, calls=%fused_computation.7 | loop fusion | flops 4193792 | bytes 6293504 | tf_op jit(solution)/shard_map/reduce_sum | solution.py:96
  287.7 0.0 copy-done
  287.7 0.5 copy-done.1
  288.2 1.5 fusion.18
  (7 shorter events, 0.1 us)
Async XLA Ops:
  0.0 287.7 %copy-start = (bf16[256,2048]{1,0:T(8,128)(2,1)S(1)}, bf16[256,2048]{1,0:T(8,128)(2,1)}, u32[]{:S(2)}) copy-start(bf16[256,2048]{1,0:T(8,128)(2,1)} %param.6) | copy-start | bytes 3145732
  0.0 10.3 %copy-start.2 = (bf16[512,2048]{1,0:T(8,128)(2,1)S(1)}, bf16[512,2048]{1,0:T(8,128)(2,1)}, u32[]{:S(2)}) copy-start(bf16[512,2048]{1,0:T(8,128)(2,1)} %param.5) | copy-start | bytes 6291460
  0.9 9.4 %collective-permute-start = (bf16[3,2048]{1,0:T(4,128)(2,1)S(1)}, bf16[3,2048]{1,0:T(4,128)(2,1)S(1)}, u32[]{:S(2)}, u32[]{:S(2)}) collective-permute-start(bf16[3,2048]{1,0:T(4,128)(2,1)S(1)} %slice.24), channel_id=1, source_target_pairs={{0,1},{1,2},{2,3},{3,4},{4,5},{5,6},{6,7},{7,8},{8,9},{9,10},{10,1... | collective-permute-start | bytes 36872 | tf_op jit(solution)/shard_map/ppermute | solution.py:12
  38.7 192.9 %all-to-all-start = ((bf16[16,2,128,8,128]{4,2,3,1,0:T(8,128)(2,1)}), bf16[16,2,128,8,128]{4,2,3,1,0:T(8,128)(2,1)}, u32[]{:S(2)}, u32[]{:S(2)}) async-start(bf16[16,2,128,8,128]{4,2,3,1,0:T(8,128)(2,1)} %stack.5), calls=%async_computation | async-start | bytes 16777216 | tf_op jit(solution)/shard_map/all_to_all | solution.py:64
  251.8 2.6 copy-start.5
  251.8 2.6 copy-start.6
  254.3 3.0 %copy-start.3 = (bf16[2048,8,128]{0,2,1:T(8,128)(2,1)S(1)}, bf16[2048,8,128]{0,2,1:T(8,128)(2,1)}, u32[]{:S(2)}) copy-start(bf16[2048,8,128]{0,2,1:T(8,128)(2,1)} %squeeze.6) | copy-start | bytes 12582916
  257.4 2.2 copy-start.4
  284.7 3.4 %copy-start.1 = (f32[512,2048]{1,0:T(8,128)S(1)}, f32[512,2048]{1,0:T(8,128)}, u32[]{:S(2)}) copy-start(f32[512,2048]{1,0:T(8,128)} %reshape.110) | copy-start | bytes 12582916
